TPU v7x, 256 devices: a whole 4x4x8 slice. The times are simulated.
256 devices in a mesh: dom: 16 (over z, x_lo), ref: 16 (over x_hi, y, core).
Axes of the slice: x: 4 (x_hi: 2, x_lo: 2; x = x_hi * 2 + x_lo), y: 4, z: 8, core: 2. Of those that a mesh axis runs over, the one named last changes fastest.
Arguments:
- particles: float32 [8192, 128], P('dom'), may hold values from -1.2 to 1.2
- references: float32 [16384, 128], P('ref'), may hold values from -1 to 1.2
Outputs:
- moved: float32 [8192, 128], P(('dom', 'ref'))
- drift: float32 [8192, 128], P(('dom', 'ref'))
All inputs are finite; a program needn't handle non-finite values.
Results may differ from a plain program's by a relative error of at most 0.00035.
Values sent between devices are 32-bit elements; how exact they have to be, the bound alone decides.
A program may use at most 64 MiB of HBM per device.

v0:
```python
import jax
import jax.numpy as jnp
from jax import lax
from jax.sharding import PartitionSpec as P

STEPS = 2


step_size = 0.5


def kernel_terms(block, others):
    inner = jnp.dot(
        block, others.T, precision=lax.Precision.HIGHEST, preferred_element_type=jnp.float32
    )
    squared = (
        jnp.sum(block * block, axis=1)[:, None]
        + jnp.sum(others * others, axis=1)[None, :]
        - 2.0 * inner
    )
    weights = jnp.exp(-0.5 * squared)
    pulled = jnp.dot(
        weights, others, precision=lax.Precision.HIGHEST, preferred_element_type=jnp.float32
    )
    return (pulled, jnp.sum(weights, axis=1))


def partial_gradient(block, own_rows, references, count_p, count_r):
    pulled, summed = kernel_terms(block, lax.all_gather(own_rows, "dom", axis=0, tiled=True))
    pull_r, sum_r = kernel_terms(block, references)
    return (pulled - summed[:, None] * block) / count_p - (
        pull_r - sum_r[:, None] * block
    ) / count_r


def on_device(particles, references):
    n_ref = lax.axis_size("ref")
    n_dom = lax.axis_size("dom")
    rows = particles.shape[0] // n_ref
    count_p = particles.shape[0] * n_dom
    count_r = references.shape[0] * n_ref
    offset = lax.axis_index("ref") * rows
    start_rows = lax.dynamic_slice_in_dim(particles, offset, rows, 0)
    block = particles
    own_rows = start_rows
    for step in range(STEPS):
        partial_value = partial_gradient(block, own_rows, references, count_p, count_r)
        gradient = lax.psum(partial_value, "ref")
        block = block - step_size * gradient
        own_rows = lax.dynamic_slice_in_dim(block, offset, rows, 0)
    return (own_rows, (own_rows - start_rows) / step_size)


def solution(mesh):
    placed = (P("dom", None), P("ref", None))
    return jax.shard_map(
        on_device,
        mesh=mesh,
        in_specs=placed,
        out_specs=(P(("dom", "ref"), None), P(("dom", "ref"), None)),
        check_vma=False,
    )
```

profile of v0, /device:TPU:1, one launch (start us, length us, event | category | flops | bytes accessed | tf_op | source)
XLA Modules:
  0.0 391.9 jit_solution(12961687768505106673)
XLA Ops:
  7.2 0.0 copy-start.1
  7.2 0.0 all-reduce.3.cloned.1.call-start
  7.2 1.2 multiply_reduce_fusion.4
  8.4 1.2 multiply_reduce_fusion
  9.7 0.7 constant_dynamic-slice_fusion.1
  10.4 31.7 %all_gather.6 = f32[512,128]{1,0:T(8,128)S(1)} all-gather(f32[32,128]{1,0:T(8,128)S(1)} %constant_dynamic-slice_fusion.1), channel_id=1, replica_groups=mesh['dom'=16,'ref'=16] {'dom'}, dimensions={0}, use_global_device_ids=true | all-gather | bytes 278528 | tf_op jit(solution)/shard_map/all_gather | solution.py:29
  42.1 0.1 multiply_reduce_fusion.3
  42.2 2.1 fusion.15
  44.4 2.3 fusion.16
  46.7 1.8 fusion.12
  48.5 2.5 fusion.9
  51.0 0.0 all-reduce.3.cloned.1.call-update
  51.1 0.0 all-reduce.5.cloned.1.call-start
  51.1 148.4 %all-reduce.3.cloned.1.call-done = f32[512,128]{1,0:T(8,128)} async-done(((f32[512,128]{1,0:T(8,128)}), f32[512,128]{1,0:T(8,128)}) %all-reduce.3.cloned.1.call-update) | async-done | bytes 262160 | tf_op jit(solution)/shard_map/psum | solution.py:48
  199.5 1.1 multiply_reduce_fusion.2
  200.7 27.7 %all_gather.7 = f32[512,128]{1,0:T(8,128)S(1)} all-gather(f32[32,128]{1,0:T(8,128)S(1)} %constant_dynamic-slice_fusion), channel_id=1, replica_groups=mesh['dom'=16,'ref'=16] {'dom'}, dimensions={0}, use_global_device_ids=true | all-gather | bytes 278528 | tf_op jit(solution)/shard_map/all_gather | solution.py:29
  228.4 0.1 multiply_reduce_fusion.1
  228.5 2.3 fusion.18
  230.8 1.2 fusion.17
  232.1 1.8 fusion.11
  233.9 2.5 fusion.10
  236.4 0.0 all-reduce.5.cloned.1.call-update
  236.5 147.3 %all-reduce.5.cloned.1.call-done = f32[512,128]{1,0:T(8,128)} async-done(((f32[512,128]{1,0:T(8,128)}), f32[512,128]{1,0:T(8,128)}) %all-reduce.5.cloned.1.call-update) | async-done | bytes 262160 | tf_op jit(solution)/shard_map/psum | solution.py:48
  383.7 1.3 subtract_multiply_fusion
  (4 shorter events, 0.0 us)
Async XLA Ops:
  7.2 37.2 %copy-start = (f32[512,128]{1,0:T(8,128)S(1)}, f32[512,128]{1,0:T(8,128)}, u32[]{:S(2)}) copy-start(f32[512,128]{1,0:T(8,128)} %param.2) | copy-start | bytes 786436
  7.2 37.2 %copy-start.1 = (f32[1024,128]{1,0:T(8,128)S(1)}, f32[1024,128]{1,0:T(8,128)}, u32[]{:S(2)}) copy-start(f32[1024,128]{1,0:T(8,128)} %param.3) | copy-start | bytes 1572868
  7.2 192.4 %all-reduce.3.cloned.1.call-start = ((), (), s32[]{:S(2)}) async-start(), calls=%async_computation | async-start | bytes 524288 | tf_op jit(solution)/shard_map/psum | solution.py:48
  51.1 332.7 %all-reduce.5.cloned.1.call-start = ((), (), s32[]{:S(2)}) async-start(), calls=%async_computation.1 | async-start | bytes 524288 | tf_op jit(solution)/shard_map/psum | solution.py:48
Sparse Core Ops, SparseCore 0:
  51.2 148.3 all-reduce.2
  236.6 147.0 all-reduce.4
where the time goes:
time: 392 us
  waiting for transfers between devices  296 us (76%)
  blocking collectives  59.4 us (15%)
  matrix products  16.7 us (4%)
  between operations  14.1 us (4%)
  other arithmetic  5.12 us (1%)
    psum x2, waiting for transfers between devices, on_device(): gradient = lax.psum(partial_value, 'ref')  296 us
    all_gather x2, blocking collectives, partial_gradient(): lax.all_gather(own_rows, 'dom', axis=0, tiled=True)  59.4 us
    dot_general x4, matrix products, kernel_terms(): jnp.dot(weights, others, precision=lax.Precision.HIGHEST, preferred_eleme...  8.73 us
    dot_general x4, matrix products, kernel_terms(): jnp.dot(block, others.T, precision=lax.Precision.HIGHEST, preferred_eleme...  7.95 us
  transfers between devices with their start and end apart: 2, of which 2 were waited for; matrix products, arithmetic and copies ran while one was open for 0% of the time, Pallas kernels for 0%

commit v1 on v0

v1 whole, which is shorter than its diff:
```python
import math

import jax
import jax.numpy as jnp
from jax import lax
from jax.experimental import pallas as pl
from jax.experimental.pallas import tpu as pltpu
from jax.sharding import PartitionSpec as P

MESH = pl.DeviceIdType.MESH
F32, BF16 = jnp.float32, jnp.bfloat16
LOG2E = math.log2(math.e)

NDOM, NREFD = 16, 16
ROWS, WIDTH = 32, 128
BLOCK = ROWS * NREFD
REFS = 1024
STEP = 0.5
COUNT_P, COUNT_R = 8192, 16384

DOM_OFFSETS = [(z, x) for z in (4, 3, 5, 2, 6, 1, 7, 0) for x in (1, 0) if (z, x) != (0, 0)]
REF_OFFSETS = [
    (x, y, c) for x in (1, 0) for y in (2, 1, 3, 0) for c in (1, 0) if (x, y, c) != (0, 0, 0)
]


def dom_partner(d, offset):
    z, x = d // 2, d % 2
    return ((z + offset[0]) % 8) * 2 + (x + offset[1]) % 2


def ref_partner(r, offset):
    x, y, c = r // 8, (r // 2) % 4, r % 2
    return ((x + offset[0]) % 2) * 8 + ((y + offset[1]) % 4) * 2 + (c + offset[2]) % 2


def split(x):
    hi = x.astype(BF16)
    return hi, (x - hi.astype(F32)).astype(BF16)


def extra(norm, ones_first):
    lane = lax.broadcasted_iota(jnp.int32, (norm.shape[0], 128), 1)
    n1 = norm.astype(BF16).astype(F32)
    rest = norm - n1
    n2 = rest.astype(BF16).astype(F32)
    n3 = rest - n2
    at, one = (3, 0) if ones_first else (0, 3)
    out = jnp.where((lane >= one) & (lane < one + 3), 1.0, 0.0)
    out = jnp.where(lane == at, n1, out)
    out = jnp.where(lane == at + 1, n2, out)
    return jnp.where(lane == at + 2, n3, out).astype(BF16)


def source_operand(x):
    hi, lo = split(x)
    norm = jnp.sum(x * x, axis=1, keepdims=True) * (-0.5 * LOG2E)
    return jnp.concatenate([hi, lo, hi, extra(norm, False)], axis=1)


def target_operand(x):
    hi, lo = split(x * LOG2E)
    norm = jnp.sum(x * x, axis=1, keepdims=True) * (-0.5 * LOG2E)
    return jnp.concatenate([hi, hi, lo, extra(norm, True)], axis=1)


def pair_terms(a, s_ref, start, size):
    src = s_ref[pl.ds(start, size), :]
    expo = lax.dot_general(a, src, (((1,), (1,)), ((), ())), preferred_element_type=F32)
    w = jnp.exp2(expo)
    w_hi = w.astype(BF16)
    w_lo = (w - w_hi.astype(F32)).astype(BF16)
    one = jnp.dot(w_hi, src[:, :256], preferred_element_type=F32)
    two = jnp.dot(w_lo, src[:, :128], preferred_element_type=F32)
    sums = w[:, :128]
    for c in range(1, size // 128):
        sums = sums + w[:, c * 128 : (c + 1) * 128]
    return one[:, :128] + one[:, 128:] + two, sums


def kernel(
    p_hbm, r_hbm, moved_ref, drift_ref,
    p_v, r_v, aop, rop, sop, grad, lanes, part, own, g_b, g_a, rs,
    in_sem, b_send, b_recv, a_send, a_recv, rs_send, rs_recv,
):
    d, r = lax.axis_index("dom"), lax.axis_index("ref")
    copy_p = pltpu.make_async_copy(p_hbm, p_v, in_sem.at[0])
    copy_r = pltpu.make_async_copy(r_hbm, r_v, in_sem.at[1])
    copy_p.start()
    copy_r.start()

    barrier = pltpu.get_barrier_semaphore()
    for off in DOM_OFFSETS:
        pl.semaphore_signal(barrier, 1, device_id={"dom": dom_partner(d, off)}, device_id_type=MESH)
    for off in REF_OFFSETS:
        pl.semaphore_signal(barrier, 1, device_id={"ref": ref_partner(r, off)}, device_id_type=MESH)

    def b_copy(step, src, off):
        q = dom_partner(d, off)
        send = pltpu.make_async_remote_copy(
            src, g_b.at[step, d], b_send.at[step, q], b_recv.at[step, d],
            device_id={"dom": q}, device_id_type=MESH,
        )
        recv = pltpu.make_async_remote_copy(
            src, g_b.at[step, q], b_send.at[step, q], b_recv.at[step, q],
            device_id={"dom": q}, device_id_type=MESH,
        )
        return q, send, recv

    def a_copy(src, off):
        q = ref_partner(r, off)
        send = pltpu.make_async_remote_copy(
            src, g_a.at[r], a_send.at[q], a_recv.at[r],
            device_id={"ref": q}, device_id_type=MESH,
        )
        recv = pltpu.make_async_remote_copy(
            src, g_a.at[q], a_send.at[q], a_recv.at[q],
            device_id={"ref": q}, device_id_type=MESH,
        )
        return q, send, recv

    def rs_copy(step, off):
        q = ref_partner(r, off)
        send = pltpu.make_async_remote_copy(
            part.at[step, q], rs.at[step, r], rs_send.at[step, q], rs_recv.at[step, r],
            device_id={"ref": q}, device_id_type=MESH,
        )
        recv = pltpu.make_async_remote_copy(
            part.at[step, r], rs.at[step, q], rs_send.at[step, q], rs_recv.at[step, q],
            device_id={"ref": q}, device_id_type=MESH,
        )
        return q, send, recv

    def refs_part(rows):
        a = aop[rows, :]
        acc, sums = pair_terms(a, rop, 0, 512)
        acc2, sums2 = pair_terms(a, rop, 512, 512)
        grad[rows, :] = -0.5 * (acc + acc2)
        lanes[rows, :] = -0.5 * (sums + sums2)

    def particles_part(rows, x):
        acc, sums = pair_terms(aop[rows, :], sop, 0, 512)
        total = jnp.sum(lanes[rows, :] + sums, axis=1, keepdims=True)
        return grad[rows, :] + acc - total * x

    def half(i):
        return pl.ds(i * 256, 256)

    def exchange(step, x_of):
        for i in range(2):
            value = particles_part(half(i), x_of(i))
            part[step, pl.ds(i * 8, 8)] = value.reshape(8, ROWS, WIDTH)
        copies = [rs_copy(step, off) for off in REF_OFFSETS]
        for _, send, _ in copies:
            send.start()
        total = part[step, r]
        for q, _, recv in copies[::-1]:
            recv.wait_recv()
            total = total + rs[step, q]
        return total * (STEP / COUNT_P), [c[1] for c in copies]

    pending = []

    copy_p.wait()
    for i in range(2):
        aop[half(i), :] = target_operand(p_v[half(i), :])
    copy_r.wait()
    for i in range(4):
        rop[half(i), :] = source_operand(r_v[half(i), :])
    pl.semaphore_wait(barrier, len(DOM_OFFSETS) + len(REF_OFFSETS))
    mine = pl.ds(pl.multiple_of(r * ROWS, ROWS), ROWS)
    copies = [b_copy(0, p_v.at[mine], off) for off in DOM_OFFSETS]
    for _, send, _ in copies:
        send.start()
        pending.append(send)
    for i in range(2):
        refs_part(half(i))
    start = p_v[mine, :]
    sop[pl.ds(pl.multiple_of(d * ROWS, ROWS), ROWS), :] = source_operand(start)
    for q, _, recv in copies[::-1]:
        recv.wait_recv()
        sop[pl.ds(pl.multiple_of(q * ROWS, ROWS), ROWS), :] = source_operand(g_b[0, q])
    delta, sends = exchange(0, lambda i: p_v[half(i), :])
    pending += sends
    now = start - delta
    own[...] = now

    a_copies = [a_copy(own, off) for off in REF_OFFSETS]
    b_copies = [b_copy(1, own, off) for off in DOM_OFFSETS]
    for c in a_copies + b_copies:
        c[1].start()
        pending.append(c[1])
    g_a[r] = now
    aop[mine, :] = target_operand(now)
    sop[pl.ds(pl.multiple_of(d * ROWS, ROWS), ROWS), :] = source_operand(now)
    for q, _, recv in a_copies[::-1]:
        recv.wait_recv()
        aop[pl.ds(pl.multiple_of(q * ROWS, ROWS), ROWS), :] = target_operand(g_a[q])
    for i in range(2):
        refs_part(half(i))
    for q, _, recv in b_copies[::-1]:
        recv.wait_recv()
        sop[pl.ds(pl.multiple_of(q * ROWS, ROWS), ROWS), :] = source_operand(g_b[1, q])
    delta, sends = exchange(1, lambda i: g_a[pl.ds(i * 8, 8)].reshape(256, WIDTH))
    pending += sends
    final = now - delta
    moved_ref[...] = final
    drift_ref[...] = (final - start) * (1.0 / STEP)
    for send in pending:
        send.wait_send()


def on_device(particles, references):
    vmem = pl.BlockSpec(memory_space=pltpu.VMEM)
    anywhere = pl.BlockSpec(memory_space=pl.ANY)
    piece = jax.ShapeDtypeStruct((ROWS, WIDTH), F32)
    return pl.pallas_call(
        kernel,
        out_shape=(piece, piece),
        in_specs=[anywhere, anywhere],
        out_specs=(vmem, vmem),
        scratch_shapes=[
            pltpu.VMEM((BLOCK, WIDTH), F32),
            pltpu.VMEM((REFS, WIDTH), F32),
            pltpu.VMEM((BLOCK, 512), BF16),
            pltpu.VMEM((REFS, 512), BF16),
            pltpu.VMEM((NDOM * ROWS, 512), BF16),
            pltpu.VMEM((BLOCK, WIDTH), F32),
            pltpu.VMEM((BLOCK, WIDTH), F32),
            pltpu.VMEM((2, NREFD, ROWS, WIDTH), F32),
            pltpu.VMEM((ROWS, WIDTH), F32),
            pltpu.VMEM((2, NDOM, ROWS, WIDTH), F32),
            pltpu.VMEM((NREFD, ROWS, WIDTH), F32),
            pltpu.VMEM((2, NREFD, ROWS, WIDTH), F32),
            pltpu.SemaphoreType.DMA((2,)),
            pltpu.SemaphoreType.DMA((2, NDOM)),
            pltpu.SemaphoreType.DMA((2, NDOM)),
            pltpu.SemaphoreType.DMA((NREFD,)),
            pltpu.SemaphoreType.DMA((NREFD,)),
            pltpu.SemaphoreType.DMA((2, NREFD)),
            pltpu.SemaphoreType.DMA((2, NREFD)),
        ],
        compiler_params=pltpu.CompilerParams(collective_id=0, has_side_effects=True),
        name="flow",
    )(particles, references)


def solution(mesh):
    return jax.shard_map(
        on_device,
        mesh=mesh,
        in_specs=(P("dom", None), P("ref", None)),
        out_specs=(P(("dom", "ref"), None), P(("dom", "ref"), None)),
        check_vma=False,
    )
```

time: 392 us -> 48.5 us (0.12)
  waiting for transfers between devices: 296 us -> 0 us
  blocking collectives: 59.4 us -> 0 us
  Pallas kernels: 0 us -> 45.8 us
  matrix products: 16.7 us -> 0 us
  between operations: 14.1 us -> 0.65 us
  other arithmetic: 5.12 us -> 0 us
    psum x2 -> x0, waiting for transfers between devices: 296 us -> none  [on_device(): gradient = lax.psum(partial_value, 'ref')]
    all_gather x2 -> x0, blocking collectives: 59.4 us -> none  [partial_gradient(): lax.all_gather(own_rows, 'dom', axis=0, tiled=True)]
    pallas_call x0 -> x1, Pallas kernels: none -> 45.8 us  [on_device(): pl.pallas_call(kernel, out_shape=(piece, piece), in_specs=[anywhere, anyw...]
    dot_general x8 -> x0, matrix products: 16.7 us -> none  [the longest x4 8.73 us: kernel_terms(): jnp.dot(weights, others, precision=lax.Precision.HIGHEST, preferred_eleme...]
  transfers between devices with their start and end apart: 2 -> 0, of which waited for: 2 -> 0; matrix products, arithmetic and copies ran while one was open for 0% -> 0% of each run, Pallas kernels for 0% -> 0%
where the time goes in v1:
time: 48.5 us; the launch traced here: 48.4 us
  Pallas kernels  45.8 us (94%)
  local copies, waits for them, and re-layouts  1.94 us (4%)
  between operations  0.65 us (1%)
    pallas_call x1, Pallas kernels, on_device(): pl.pallas_call(kernel, out_shape=(piece, piece), in_specs=[anywhere, anyw...  45.8 us
    unnamed x4, local copies, waits for them, and re-layouts  1.94 us

profile of v1, /device:TPU:1, one launch (start us, length us, event | category | flops | bytes accessed | tf_op | source)
XLA Modules:
  0.0 48.4 jit_solution(7517845802393844073)
XLA Ops:
  0.6 45.8 %flow.1 = (f32[32,128]{1,0:T(8,128)}, f32[32,128]{1,0:T(8,128)}) custom-call(f32[512,128]{1,0:T(8,128)} %p_hbm.1, f32[1024,128]{1,0:T(8,128)} %r_hbm.1), custom_call_target="tpu_custom_call" | custom-call | tf_op jit(solution)/shard_map/flow/pallas_call | solution.py:217
  46.4 0.0 copy-start
  46.5 1.3 %copy.6 = f32[32,128]{1,0:T(8,128)} copy(f32[32,128]{1,0:T(8,128)} %get-tuple-element.4) | data formatting | bytes 32768
  47.8 0.0 copy-done
  47.8 0.6 %copy.7 = f32[32,128]{1,0:T(8,128)} copy(f32[32,128]{1,0:T(8,128)S(1)} %copy-done) | data formatting | bytes 32768
Async XLA Ops:
  46.4 1.3 %copy-start = (f32[32,128]{1,0:T(8,128)S(1)}, f32[32,128]{1,0:T(8,128)}, u32[]{:S(2)}) copy-start(f32[32,128]{1,0:T(8,128)} %get-tuple-element.5) | copy-start | bytes 49156

commit v2 on v1

v2 whole, which is shorter than its diff:
```python
import math

import jax
import jax.numpy as jnp
from jax import lax
from jax.experimental import pallas as pl
from jax.experimental.pallas import tpu as pltpu
from jax.sharding import PartitionSpec as P

MESH = pl.DeviceIdType.MESH
F32, BF16 = jnp.float32, jnp.bfloat16
LOG2E = math.log2(math.e)

NDOM, NREFD = 16, 16
ROWS, WIDTH = 32, 128
BLOCK = ROWS * NREFD
REFS = 1024
STEP = 0.5
COUNT_P, COUNT_R = 8192, 16384

DOM_SLOTS = [(0, 0), (0, 1), (1, 0), (7, 0), (1, 1), (7, 1), (2, 0), (6, 0)]
DOM_SLOTS += [(2, 1), (6, 1), (3, 0), (5, 0), (3, 1), (5, 1), (4, 0), (4, 1)]
REF_SLOTS = [(0, 0, 0), (0, 0, 1)] + [(0, y, c) for y in (1, 3, 2) for c in (0, 1)]
REF_SLOTS += [(1, y, c) for y in (0, 1, 3, 2) for c in (0, 1)]


def dom_partner(d, slot):
    dz, dx = DOM_SLOTS[slot]
    return ((d // 2 + dz) % 8) * 2 + (d % 2 + dx) % 2


def ref_partner(r, slot):
    dx, dy, dc = REF_SLOTS[slot]
    return ((r // 8 + dx) % 2) * 8 + (((r // 2) % 4 + dy) % 4) * 2 + (r % 2 + dc) % 2


def dom_back(slot):
    dz, dx = DOM_SLOTS[slot]
    return DOM_SLOTS.index((-dz % 8, dx))


def ref_back(slot):
    dx, dy, dc = REF_SLOTS[slot]
    return REF_SLOTS.index((dx, -dy % 4, dc))


def split(x):
    hi = x.astype(BF16)
    return hi, (x - hi.astype(F32)).astype(BF16)


def extra(norm, ones_first):
    lane = lax.broadcasted_iota(jnp.int32, (norm.shape[0], 128), 1)
    n1 = norm.astype(BF16).astype(F32)
    rest = norm - n1
    n2 = rest.astype(BF16).astype(F32)
    n3 = rest - n2
    at, one = (3, 0) if ones_first else (0, 3)
    out = jnp.where((lane >= one) & (lane < one + 3), 1.0, 0.0)
    out = jnp.where(lane == at, n1, out)
    out = jnp.where(lane == at + 1, n2, out)
    return jnp.where(lane == at + 2, n3, out).astype(BF16)


def source_operand(x):
    hi, lo = split(x)
    norm = jnp.sum(x * x, axis=1, keepdims=True) * (-0.5 * LOG2E)
    return jnp.concatenate([hi, lo, hi, extra(norm, False)], axis=1)


def target_operand(x):
    hi, lo = split(x * LOG2E)
    norm = jnp.sum(x * x, axis=1, keepdims=True) * (-0.5 * LOG2E)
    return jnp.concatenate([hi, hi, lo, extra(norm, True)], axis=1)


def pair_terms(a, s_ref, start, size):
    src = s_ref[pl.ds(start, size), :]
    expo = lax.dot_general(a, src, (((1,), (1,)), ((), ())), preferred_element_type=F32)
    w = jnp.exp2(expo)
    w_hi = w.astype(BF16)
    w_lo = (w - w_hi.astype(F32)).astype(BF16)
    one = jnp.dot(w_hi, src[:, :256], preferred_element_type=F32)
    two = jnp.dot(w_lo, src[:, :128], preferred_element_type=F32)
    sums = w[:, :128]
    for c in range(1, size // 128):
        sums = sums + w[:, c * 128 : (c + 1) * 128]
    return one[:, :128] + one[:, 128:] + two, sums


def kernel(
    p_hbm, r_hbm, out_ref,
    p_v, r_v, xs, aop, rop, sop, grad, lanes, part, own, g_b, g_a, rs,
    in_sem, b_send, b_recv, a_send, a_recv, rs_send, rs_recv,
):
    d, r = lax.axis_index("dom"), lax.axis_index("ref")
    mine = pl.ds(pl.multiple_of(r * ROWS, ROWS), ROWS)
    copy_own = pltpu.make_async_copy(p_hbm.at[mine], own.at[0], in_sem.at[0])
    copy_p = pltpu.make_async_copy(p_hbm, p_v, in_sem.at[1])
    copy_r = pltpu.make_async_copy(r_hbm, r_v, in_sem.at[2])
    copy_own.start()
    copy_p.start()
    copy_r.start()

    barrier = pltpu.get_barrier_semaphore()
    for slot in range(15, 0, -1):
        device = {"dom": dom_partner(d, slot)}
        pl.semaphore_signal(barrier, 1, device_id=device, device_id_type=MESH)
    for slot in range(15, 0, -1):
        device = {"ref": ref_partner(r, slot)}
        pl.semaphore_signal(barrier, 1, device_id=device, device_id_type=MESH)

    def dom_copy(src, dst, send, recv, slot, to):
        return pltpu.make_async_remote_copy(
            src, dst.at[to], send.at[slot], recv.at[to],
            device_id={"dom": dom_partner(d, slot)}, device_id_type=MESH,
        )

    def ref_copy(src, dst, send, recv, slot, to):
        return pltpu.make_async_remote_copy(
            src, dst.at[to], send.at[slot], recv.at[to],
            device_id={"ref": ref_partner(r, slot)}, device_id_type=MESH,
        )

    pending = []

    def send_b(step):
        for slot in range(15, 0, -1):
            args = own.at[step], g_b.at[step], b_send.at[step], b_recv.at[step]
            copy = dom_copy(*args, slot, dom_back(slot))
            copy.start()
            pending.append(copy)

    def wait_b(step, slots):
        for slot in slots:
            args = own.at[step], g_b.at[step], b_send.at[step], b_recv.at[step]
            dom_copy(*args, slot, slot).wait_recv()

    def send_a():
        for slot in range(15, 0, -1):
            copy = ref_copy(own.at[1], g_a, a_send, a_recv, slot, ref_back(slot))
            copy.start()
            pending.append(copy)

    def wait_a(slots):
        for slot in slots:
            ref_copy(own.at[1], g_a, a_send, a_recv, slot, slot).wait_recv()

    def send_rs(step, slots):
        for slot in slots:
            args = part.at[step, slot], rs.at[step], rs_send.at[step], rs_recv.at[step]
            copy = ref_copy(*args, slot, ref_back(slot))
            copy.start()
            pending.append(copy)

    def wait_rs(step):
        for slot in range(1, 16):
            args = part.at[step, slot], rs.at[step], rs_send.at[step], rs_recv.at[step]
            ref_copy(*args, slot, slot).wait_recv()
        total = part[step, 0] + rs[step, 1]
        for slot in range(2, 16):
            total = total + rs[step, slot]
        return total * (STEP / COUNT_P)

    near, far = pl.ds(0, 256), pl.ds(256, 256)

    def refs_part(rows):
        a = aop[rows, :]
        acc, sums = pair_terms(a, rop, 0, 512)
        acc2, sums2 = pair_terms(a, rop, 512, 512)
        grad[rows, :] = -0.5 * (acc + acc2)
        lanes[rows, :] = -0.5 * (sums + sums2)

    def near_part(rows):
        acc, sums = pair_terms(aop[rows, :], sop, 0, 256)
        grad[rows, :] += acc
        lanes[rows, :] += sums

    def far_part(step, rows):
        acc, sums = pair_terms(aop[rows, :], sop, 256, 256)
        total = jnp.sum(lanes[rows, :] + sums, axis=1, keepdims=True)
        value = grad[rows, :] + acc - total * xs[rows, :]
        part[step, pl.ds(rows.start // ROWS, 8)] = value.reshape(8, ROWS, WIDTH)

    def prep_b(step, rows):
        pieces = g_b[step, pl.ds(rows.start // ROWS, 8)]
        sop[rows, :] = source_operand(pieces.reshape(256, WIDTH))

    def finish(step):
        wait_b(step, range(8, 16))
        prep_b(step, far)
        far_part(step, far)
        send_rs(step, range(15, 7, -1))
        far_part(step, near)
        send_rs(step, range(7, 0, -1))
        return wait_rs(step)

    copy_own.wait()
    pl.semaphore_wait(barrier, 30)
    send_b(0)
    start = own[0]
    g_b[0, 0] = start
    copy_p.wait()
    for slot in range(16):
        rows = pl.ds(pl.multiple_of(ref_partner(r, slot) * ROWS, ROWS), ROWS)
        xs[pl.ds(slot * ROWS, ROWS), :] = p_v[rows, :]
    for rows in (near, far):
        aop[rows, :] = target_operand(xs[rows, :])
    copy_r.wait()
    for i in range(4):
        rows = pl.ds(i * 256, 256)
        rop[rows, :] = source_operand(r_v[rows, :])
    for rows in (near, far):
        refs_part(rows)
    wait_b(0, range(1, 8))
    prep_b(0, near)
    for rows in (near, far):
        near_part(rows)
    now = start - finish(0)

    own[1] = now
    send_a()
    send_b(1)
    g_b[1, 0] = now
    g_a[0] = now
    wait_a(range(1, 8))
    xs[near, :] = g_a[pl.ds(0, 8)].reshape(256, WIDTH)
    aop[near, :] = target_operand(xs[near, :])
    refs_part(near)
    wait_b(1, range(1, 8))
    prep_b(1, near)
    near_part(near)
    wait_a(range(8, 16))
    xs[far, :] = g_a[pl.ds(8, 8)].reshape(256, WIDTH)
    aop[far, :] = target_operand(xs[far, :])
    refs_part(far)
    near_part(far)
    delta = finish(1)
    out_ref[0] = start
    out_ref[1] = now
    out_ref[2] = delta
    for copy in pending:
        copy.wait_send()


def on_device(particles, references):
    out = pl.pallas_call(
        kernel,
        out_shape=jax.ShapeDtypeStruct((3, ROWS, WIDTH), F32),
        in_specs=[pl.BlockSpec(memory_space=pl.ANY)] * 2,
        out_specs=pl.BlockSpec(memory_space=pltpu.VMEM),
        scratch_shapes=[
            pltpu.VMEM((BLOCK, WIDTH), F32),
            pltpu.VMEM((REFS, WIDTH), F32),
            pltpu.VMEM((BLOCK, WIDTH), F32),
            pltpu.VMEM((BLOCK, 512), BF16),
            pltpu.VMEM((REFS, 512), BF16),
            pltpu.VMEM((NDOM * ROWS, 512), BF16),
            pltpu.VMEM((BLOCK, WIDTH), F32),
            pltpu.VMEM((BLOCK, WIDTH), F32),
            pltpu.VMEM((2, NREFD, ROWS, WIDTH), F32),
            pltpu.VMEM((2, ROWS, WIDTH), F32),
            pltpu.VMEM((2, NDOM, ROWS, WIDTH), F32),
            pltpu.VMEM((NREFD, ROWS, WIDTH), F32),
            pltpu.VMEM((2, NREFD, ROWS, WIDTH), F32),
            pltpu.SemaphoreType.DMA((3,)),
            pltpu.SemaphoreType.DMA((2, NDOM)),
            pltpu.SemaphoreType.DMA((2, NDOM)),
            pltpu.SemaphoreType.DMA((NREFD,)),
            pltpu.SemaphoreType.DMA((NREFD,)),
            pltpu.SemaphoreType.DMA((2, NREFD)),
            pltpu.SemaphoreType.DMA((2, NREFD)),
        ],
        compiler_params=pltpu.CompilerParams(collective_id=0, has_side_effects=True),
        name="flow",
    )(particles, references)
    moved = out[1] - out[2]
    return moved, (moved - out[0]) * (1.0 / STEP)


def solution(mesh):
    return jax.shard_map(
        on_device,
        mesh=mesh,
        in_specs=(P("dom", None), P("ref", None)),
        out_specs=(P(("dom", "ref"), None), P(("dom", "ref"), None)),
        check_vma=False,
    )
```

time: 48.5 us -> 46.5 us (0.959)
  local copies, waits for them, and re-layouts: 1.94 us -> 0 us
  Pallas kernels: 45.8 us -> 44.2 us
  other arithmetic: 0 us -> 1.37 us
    unnamed x4 -> x0, local copies, waits for them, and re-layouts: 1.94 us -> none
    pallas_call x1, Pallas kernels: 45.8 us -> 44.2 us  [on_device(): pl.pallas_call(kernel, out_shape=jax.ShapeDtypeStruct((3, ROWS, WIDTH), F...]
    mul x0 -> x1, other arithmetic: none -> 1.37 us  [on_device(): return (moved, (moved - out[0]) * (1.0 / STEP))]
where the time goes in v2:
time: 46.5 us; the launch traced here: 46.3 us
  Pallas kernels  44.2 us (95%)
  other arithmetic  1.37 us (3%)
  between operations  0.64 us (1%)
    pallas_call x1, Pallas kernels, on_device(): pl.pallas_call(kernel, out_shape=jax.ShapeDtypeStruct((3, ROWS, WIDTH), F...  44.2 us
    mul x1, other arithmetic, on_device(): return (moved, (moved - out[0]) * (1.0 / STEP))  1.37 us

profile of v2, /device:TPU:1, one launch (start us, length us, event | category | flops | bytes accessed | tf_op | source)
XLA Modules:
  0.0 46.3 jit_solution(6290171697626528378)
XLA Ops:
  0.6 44.2 %flow.1 = f32[3,32,128]{2,1,0:T(8,128)} custom-call(f32[512,128]{1,0:T(8,128)} %p_hbm.1, f32[1024,128]{1,0:T(8,128)} %r_hbm.1), custom_call_target="tpu_custom_call" | custom-call | tf_op jit(solution)/shard_map/flow/pallas_call | solution.py:247
  44.9 1.4 %fusion = (f32[32,128]{1,0:T(8,128)}, f32[32,128]{1,0:T(8,128)}) fusion(f32[3,32,128]{2,1,0:T(8,128)} %flow.1), kind=kLoop, calls=%fused_computation.1 | loop fusion | flops 12288 | bytes 81920 | tf_op jit(solution)/shard_map/mul | solution.py:278

commit v3 on v2

--- a/solution.py
+++ b/solution.py
@@ -110,57 +110,40 @@
         device = {"ref": ref_partner(r, slot)}
         pl.semaphore_signal(barrier, 1, device_id=device, device_id_type=MESH)
 
-    def dom_copy(src, dst, send, recv, slot, to):
+    def dom_copy(src, dst, send, recv, slot):
+        to = dom_back(slot)
         return pltpu.make_async_remote_copy(
-            src, dst.at[to], send.at[slot], recv.at[to],
+            src, dst.at[to], send, recv.at[to // 8],
             device_id={"dom": dom_partner(d, slot)}, device_id_type=MESH,
         )
 
-    def ref_copy(src, dst, send, recv, slot, to):
+    def ref_copy(src, dst, send, recv, slot):
+        to = ref_back(slot)
         return pltpu.make_async_remote_copy(
-            src, dst.at[to], send.at[slot], recv.at[to],
+            src, dst.at[to], send, recv.at[to // 8],
             device_id={"ref": ref_partner(r, slot)}, device_id_type=MESH,
         )
 
-    pending = []
-
     def send_b(step):
         for slot in range(15, 0, -1):
-            args = own.at[step], g_b.at[step], b_send.at[step], b_recv.at[step]
-            copy = dom_copy(*args, slot, dom_back(slot))
-            copy.start()
-            pending.append(copy)
-
-    def wait_b(step, slots):
-        for slot in slots:
-            args = own.at[step], g_b.at[step], b_send.at[step], b_recv.at[step]
-            dom_copy(*args, slot, slot).wait_recv()
+            dom_copy(own.at[step], g_b.at[step], b_send.at[step], b_recv.at[step], slot).start()
 
     def send_a():
         for slot in range(15, 0, -1):
-            copy = ref_copy(own.at[1], g_a, a_send, a_recv, slot, ref_back(slot))
-            copy.start()
-            pending.append(copy)
-
-    def wait_a(slots):
-        for slot in slots:
-            ref_copy(own.at[1], g_a, a_send, a_recv, slot, slot).wait_recv()
+            ref_copy(own.at[1], g_a, a_send, a_recv, slot).start()
 
     def send_rs(step, slots):
         for slot in slots:
-            args = part.at[step, slot], rs.at[step], rs_send.at[step], rs_recv.at[step]
-            copy = ref_copy(*args, slot, ref_back(slot))
-            copy.start()
-            pending.append(copy)
-
-    def wait_rs(step):
-        for slot in range(1, 16):
-            args = part.at[step, slot], rs.at[step], rs_send.at[step], rs_recv.at[step]
-            ref_copy(*args, slot, slot).wait_recv()
-        total = part[step, 0] + rs[step, 1]
-        for slot in range(2, 16):
-            total = total + rs[step, slot]
-        return total * (STEP / COUNT_P)
+            src = part.at[step, slot]
+            ref_copy(src, rs.at[step], rs_send.at[step], rs_recv.at[step], slot).start()
+
+    def arrived(dst, recv, half):
+        pieces = dst.at[pl.ds(1, 7)] if half == 0 else dst.at[pl.ds(8, 8)]
+        pltpu.make_async_copy(pieces, pieces, recv.at[half]).wait()
+
+    def sent(dst, send):
+        pieces = dst.at[pl.ds(1, 15)]
+        pltpu.make_async_copy(pieces, pieces, send).wait()
 
     near, far = pl.ds(0, 256), pl.ds(256, 256)
 
@@ -171,29 +154,32 @@
         grad[rows, :] = -0.5 * (acc + acc2)
         lanes[rows, :] = -0.5 * (sums + sums2)
 
-    def near_part(rows):
-        acc, sums = pair_terms(aop[rows, :], sop, 0, 256)
-        grad[rows, :] += acc
-        lanes[rows, :] += sums
-
-    def far_part(step, rows):
-        acc, sums = pair_terms(aop[rows, :], sop, 256, 256)
+    def particles_part(step, rows):
+        acc, sums = pair_terms(aop[rows, :], sop, 0, 512)
         total = jnp.sum(lanes[rows, :] + sums, axis=1, keepdims=True)
         value = grad[rows, :] + acc - total * xs[rows, :]
-        part[step, pl.ds(rows.start // ROWS, 8)] = value.reshape(8, ROWS, WIDTH)
+        count = rows.size // ROWS
+        part[step, pl.ds(rows.start // ROWS, count)] = value.reshape(count, ROWS, WIDTH)
 
     def prep_b(step, rows):
         pieces = g_b[step, pl.ds(rows.start // ROWS, 8)]
         sop[rows, :] = source_operand(pieces.reshape(256, WIDTH))
 
     def finish(step):
-        wait_b(step, range(8, 16))
+        arrived(g_b.at[step], b_recv.at[step], 1)
         prep_b(step, far)
-        far_part(step, far)
+        arrived(g_b.at[step], b_recv.at[step], 0)
+        prep_b(step, near)
+        particles_part(step, far)
         send_rs(step, range(15, 7, -1))
-        far_part(step, near)
+        particles_part(step, near)
         send_rs(step, range(7, 0, -1))
-        return wait_rs(step)
+        arrived(rs.at[step], rs_recv.at[step], 0)
+        arrived(rs.at[step], rs_recv.at[step], 1)
+        total = part[step, 0]
+        for slot in range(1, 16):
+            total = total + rs[step, slot]
+        return total * (STEP / COUNT_P)
 
     copy_own.wait()
     pl.semaphore_wait(barrier, 30)
@@ -212,10 +198,6 @@
         rop[rows, :] = source_operand(r_v[rows, :])
     for rows in (near, far):
         refs_part(rows)
-    wait_b(0, range(1, 8))
-    prep_b(0, near)
-    for rows in (near, far):
-        near_part(rows)
     now = start - finish(0)
 
     own[1] = now
@@ -223,31 +205,27 @@
     send_b(1)
     g_b[1, 0] = now
     g_a[0] = now
-    wait_a(range(1, 8))
-    xs[near, :] = g_a[pl.ds(0, 8)].reshape(256, WIDTH)
-    aop[near, :] = target_operand(xs[near, :])
-    refs_part(near)
-    wait_b(1, range(1, 8))
-    prep_b(1, near)
-    near_part(near)
-    wait_a(range(8, 16))
-    xs[far, :] = g_a[pl.ds(8, 8)].reshape(256, WIDTH)
-    aop[far, :] = target_operand(xs[far, :])
-    refs_part(far)
-    near_part(far)
+    for half, rows in ((0, near), (1, far)):
+        arrived(g_a, a_recv, half)
+        xs[rows, :] = g_a[pl.ds(half * 8, 8)].reshape(256, WIDTH)
+        aop[rows, :] = target_operand(xs[rows, :])
+        refs_part(rows)
     delta = finish(1)
     out_ref[0] = start
     out_ref[1] = now
     out_ref[2] = delta
-    for copy in pending:
-        copy.wait_send()
+    for step in range(2):
+        sent(g_b.at[step], b_send.at[step])
+        sent(rs.at[step], rs_send.at[step])
+    sent(g_a, a_send)
 
 
 def on_device(particles, references):
+    inputs = [pltpu.with_memory_space_constraint(x, pltpu.HBM) for x in (particles, references)]
     out = pl.pallas_call(
         kernel,
         out_shape=jax.ShapeDtypeStruct((3, ROWS, WIDTH), F32),
-        in_specs=[pl.BlockSpec(memory_space=pl.ANY)] * 2,
+        in_specs=[pl.BlockSpec(memory_space=pltpu.HBM)] * 2,
         out_specs=pl.BlockSpec(memory_space=pltpu.VMEM),
         scratch_shapes=[
             pltpu.VMEM((BLOCK, WIDTH), F32),
@@ -264,16 +242,18 @@
             pltpu.VMEM((NREFD, ROWS, WIDTH), F32),
             pltpu.VMEM((2, NREFD, ROWS, WIDTH), F32),
             pltpu.SemaphoreType.DMA((3,)),
-            pltpu.SemaphoreType.DMA((2, NDOM)),
-            pltpu.SemaphoreType.DMA((2, NDOM)),
-            pltpu.SemaphoreType.DMA((NREFD,)),
-            pltpu.SemaphoreType.DMA((NREFD,)),
-            pltpu.SemaphoreType.DMA((2, NREFD)),
-            pltpu.SemaphoreType.DMA((2, NREFD)),
+            pltpu.SemaphoreType.DMA((2,)),
+            pltpu.SemaphoreType.DMA((2, 2)),
+            pltpu.SemaphoreType.DMA(()),
+            pltpu.SemaphoreType.DMA((2,)),
+            pltpu.SemaphoreType.DMA((2,)),
+            pltpu.SemaphoreType.DMA((2, 2)),
         ],
-        compiler_params=pltpu.CompilerParams(collective_id=0, has_side_effects=True),
+        compiler_params=pltpu.CompilerParams(
+            collective_id=0, has_side_effects=True, vmem_limit_bytes=24 << 20
+        ),
         name="flow",
-    )(particles, references)
+    )(*inputs)
     moved = out[1] - out[2]
     return moved, (moved - out[0]) * (1.0 / STEP)
 

time: 46.5 us -> 41.7 us (0.90)
  Pallas kernels: 44.2 us -> 40.2 us
  other arithmetic: 1.37 us -> 0.62 us
    pallas_call x1, Pallas kernels: 44.2 us -> 40.2 us  [on_device(): pl.pallas_call(kernel, out_shape=jax.ShapeDtypeStruct((3, ROWS, WIDTH), F...]
    mul x1, other arithmetic: 1.37 us -> 0.62 us  [on_device(): return (moved, (moved - out[0]) * (1.0 / STEP))]
where the time goes in v3:
time: 41.7 us; the launch traced here: 41.5 us
  Pallas kernels  40.2 us (96%)
  between operations  0.64 us (2%)
  other arithmetic  0.62 us (1%)
    pallas_call x1, Pallas kernels, on_device(): pl.pallas_call(kernel, out_shape=jax.ShapeDtypeStruct((3, ROWS, WIDTH), F...  40.2 us

profile of v3, /device:TPU:1, one launch (start us, length us, event | category | flops | bytes accessed | tf_op | source)
XLA Modules:
  0.0 41.5 jit_solution(13635853462907690126)
XLA Ops:
  0.6 40.2 %flow.1 = f32[3,32,128]{2,1,0:T(8,128)S(1)} custom-call(f32[512,128]{1,0:T(8,128)} %p_hbm.1, f32[1024,128]{1,0:T(8,128)} %r_hbm.1), custom_call_target="tpu_custom_call" | custom-call | tf_op jit(solution)/shard_map/flow/pallas_call | solution.py:225
  40.9 0.6 %fusion = (f32[32,128]{1,0:T(8,128)}, f32[32,128]{1,0:T(8,128)}) fusion(f32[3,32,128]{2,1,0:T(8,128)S(1)} %flow.1), kind=kLoop, calls=%fused_computation.1 | loop fusion | flops 12288 | bytes 81920 | tf_op jit(solution)/shard_map/mul | solution.py:258

commit v4 on v3

--- a/solution.py
+++ b/solution.py
@@ -18,10 +18,11 @@
 STEP = 0.5
 COUNT_P, COUNT_R = 8192, 16384
 
-DOM_SLOTS = [(0, 0), (0, 1), (1, 0), (7, 0), (1, 1), (7, 1), (2, 0), (6, 0)]
-DOM_SLOTS += [(2, 1), (6, 1), (3, 0), (5, 0), (3, 1), (5, 1), (4, 0), (4, 1)]
+DZ = (0, 1, 7, 2, 6, 3, 5, 4)
+DOM_SLOTS = [(dz, dx) for dz in DZ for dx in (0, 1)]
 REF_SLOTS = [(0, 0, 0), (0, 0, 1)] + [(0, y, c) for y in (1, 3, 2) for c in (0, 1)]
 REF_SLOTS += [(1, y, c) for y in (0, 1, 3, 2) for c in (0, 1)]
+NOWHERE = 4.0
 
 
 def dom_partner(d, slot):
@@ -42,6 +43,16 @@
 def ref_back(slot):
     dx, dy, dc = REF_SLOTS[slot]
     return REF_SLOTS.index((dx, -dy % 4, dc))
+
+
+def dom_rank(d):
+    z = d // 2
+    return (z * (8 - z) * 8 + z) * 2 + d % 2
+
+
+def ref_rank(r):
+    y = (r // 2) % 4
+    return (y * (4 - y) + 4 * (r // 8)) * 16 + r
 
 
 def split(x):
@@ -90,8 +101,8 @@
 
 def kernel(
     p_hbm, r_hbm, out_ref,
-    p_v, r_v, xs, aop, rop, sop, grad, lanes, part, own, g_b, g_a, rs,
-    in_sem, b_send, b_recv, a_send, a_recv, rs_send, rs_recv,
+    p_v, r_v, xs, aop, rop, sop, bop, asop, grad, lanes, part, own, g_b, g_a, rs, back, g_back,
+    in_sem, b_send, b_recv, back_send, back_recv, a_recv, ref_send, rs_recv, ready,
 ):
     d, r = lax.axis_index("dom"), lax.axis_index("ref")
     mine = pl.ds(pl.multiple_of(r * ROWS, ROWS), ROWS)
@@ -102,48 +113,103 @@
     copy_p.start()
     copy_r.start()
 
+    rank = dom_rank(d)
+    pairs = [(1, 1)] + [(2 * i, 2) for i in range(1, 8)]
+    dom_later = [dom_rank(dom_partner(d, first)) > rank for first, _ in pairs]
+    ref_later = [None] + [ref_rank(ref_partner(r, slot)) > ref_rank(r) for slot in range(1, 16)]
+    n_dom = sum(jnp.where(later, 0, size) for later, (_, size) in zip(dom_later, pairs))
+    n_ref = sum(jnp.where(later, 0, 1) for later in ref_later[1:])
+    far_group = d // 2 * (8 - d // 2) < 14
+
     barrier = pltpu.get_barrier_semaphore()
+    for i in (7, 6, 5, 4, 3, 2, 1, 0):
+        first, size = pairs[i]
+
+        @pl.when(dom_later[i])
+        def _():
+            for slot in range(first, first + size):
+                device = {"dom": dom_partner(d, slot)}
+                pl.semaphore_signal(barrier, 1, device_id=device, device_id_type=MESH)
+
     for slot in range(15, 0, -1):
-        device = {"dom": dom_partner(d, slot)}
-        pl.semaphore_signal(barrier, 1, device_id=device, device_id_type=MESH)
-    for slot in range(15, 0, -1):
-        device = {"ref": ref_partner(r, slot)}
-        pl.semaphore_signal(barrier, 1, device_id=device, device_id_type=MESH)
+
+        @pl.when(ref_later[slot])
+        def _():
+            device = {"ref": ref_partner(r, slot)}
+            pl.semaphore_signal(barrier, 1, device_id=device, device_id_type=MESH)
 
     def dom_copy(src, dst, send, recv, slot):
         to = dom_back(slot)
         return pltpu.make_async_remote_copy(
-            src, dst.at[to], send, recv.at[to // 8],
+            src, dst.at[to], send.at[slot // 2], recv.at[to // 2],
             device_id={"dom": dom_partner(d, slot)}, device_id_type=MESH,
         )
 
-    def ref_copy(src, dst, send, recv, slot):
+    def ref_copy(src, dst, recv, slot):
         to = ref_back(slot)
         return pltpu.make_async_remote_copy(
-            src, dst.at[to], send, recv.at[to // 8],
+            src, dst.at[to], ref_send, recv.at[to // 8],
             device_id={"ref": ref_partner(r, slot)}, device_id_type=MESH,
         )
 
+    def wait_bytes(pieces, sem):
+        pltpu.make_async_copy(pieces, pieces, sem).wait()
+
     def send_b(step):
-        for slot in range(15, 0, -1):
-            dom_copy(own.at[step], g_b.at[step], b_send.at[step], b_recv.at[step], slot).start()
+        for i in (7, 5, 6, 3, 4, 1, 2, 0):
+            first, size = pairs[i]
+
+            @pl.when(jnp.logical_not(dom_later[i]))
+            def _():
+                for slot in range(first + size - 1, first - 1, -1):
+                    dom_copy(own.at[step], g_b.at[step], b_send, b_recv.at[step], slot).start()
+
+    def send_back(step, group):
+        for i in (3, 1, 2, 0) if group == 0 else (7, 5, 6, 4):
+            first, size = pairs[i]
+
+            @pl.when(dom_later[i])
+            def _():
+                for slot in range(first + size - 1, first - 1, -1):
+                    src = back.at[step, slot]
+                    dom_copy(src, g_back.at[step], back_send, back_recv.at[step], slot).start()
+
+    def wait_b(step, group):
+        for i in range(4 * group, 4 * group + 4):
+            first, size = pairs[i]
+
+            @pl.when(dom_later[i])
+            def _():
+                wait_bytes(g_b.at[step, pl.ds(first, size)], b_recv.at[step, first // 2])
+
+    def wait_back(step):
+        for i in range(8):
+            first, size = pairs[i]
+
+            @pl.when(jnp.logical_not(dom_later[i]))
+            def _():
+                wait_bytes(g_back.at[step, pl.ds(first, size)], back_recv.at[step, first // 2])
+
+    def fill():
+        for i in range(8):
+            first, size = pairs[i]
+
+            @pl.when(jnp.logical_not(dom_later[i]))
+            def _():
+                for step in range(2):
+                    g_b[step, pl.ds(first, size)] = jnp.full((size, ROWS, WIDTH), NOWHERE, F32)
+
+            @pl.when(dom_later[i])
+            def _():
+                for step in range(2):
+                    g_back[step, pl.ds(first, size)] = jnp.zeros((size, ROWS, WIDTH), F32)
 
     def send_a():
         for slot in range(15, 0, -1):
-            ref_copy(own.at[1], g_a, a_send, a_recv, slot).start()
-
-    def send_rs(step, slots):
-        for slot in slots:
-            src = part.at[step, slot]
-            ref_copy(src, rs.at[step], rs_send.at[step], rs_recv.at[step], slot).start()
+            ref_copy(own.at[1], g_a, a_recv, slot).start()
 
     def arrived(dst, recv, half):
-        pieces = dst.at[pl.ds(1, 7)] if half == 0 else dst.at[pl.ds(8, 8)]
-        pltpu.make_async_copy(pieces, pieces, recv.at[half]).wait()
-
-    def sent(dst, send):
-        pieces = dst.at[pl.ds(1, 15)]
-        pltpu.make_async_copy(pieces, pieces, send).wait()
+        wait_bytes(dst.at[pl.ds(1, 7)] if half == 0 else dst.at[pl.ds(8, 8)], recv.at[half])
 
     near, far = pl.ds(0, 256), pl.ds(256, 256)
 
@@ -154,44 +220,97 @@
         grad[rows, :] = -0.5 * (acc + acc2)
         lanes[rows, :] = -0.5 * (sums + sums2)
 
-    def particles_part(step, rows):
-        acc, sums = pair_terms(aop[rows, :], sop, 0, 512)
-        total = jnp.sum(lanes[rows, :] + sums, axis=1, keepdims=True)
-        value = grad[rows, :] + acc - total * xs[rows, :]
-        count = rows.size // ROWS
-        part[step, pl.ds(rows.start // ROWS, count)] = value.reshape(count, ROWS, WIDTH)
-
-    def prep_b(step, rows):
-        pieces = g_b[step, pl.ds(rows.start // ROWS, 8)]
-        sop[rows, :] = source_operand(pieces.reshape(256, WIDTH))
+    def prep_a(rows):
+        x = xs[rows, :]
+        aop[rows, :] = target_operand(x)
+
+    def prep_b(step, group):
+        rows = near if group == 0 else far
+        x = g_b[step, pl.ds(group * 8, 8)].reshape(256, WIDTH)
+        sop[rows, :] = source_operand(x)
+        bop[rows, :] = target_operand(x)
+
+    def forward(group):
+        for rows in (far, near):
+            acc, sums = pair_terms(aop[rows, :], sop, group * 256, 256)
+            grad[rows, :] += acc
+            lanes[rows, :] += sums
+
+    def reverse(step, group):
+        rows, slots = (near, far)[group], pl.ds(group * 8, 8)
+        acc, sums = pair_terms(bop[rows, :], asop, 0, 512)
+        x = g_b[step, slots].reshape(256, WIDTH)
+        value = acc - jnp.sum(sums, axis=1, keepdims=True) * x
+        back[step, slots] = value.reshape(8, ROWS, WIDTH)
+
+    def send_rs(step):
+        for rows, slots, order in ((far, pl.ds(8, 8), range(15, 7, -1)), (near, pl.ds(0, 8), range(7, 0, -1))):
+            total = jnp.sum(lanes[rows, :], axis=1, keepdims=True)
+            value = grad[rows, :] - total * xs[rows, :]
+            part[step, slots] = value.reshape(8, ROWS, WIDTH)
+            for slot in order:
+                ref_copy(part.at[step, slot], rs.at[step], rs_recv.at[step], slot).start()
 
     def finish(step):
-        arrived(g_b.at[step], b_recv.at[step], 1)
-        prep_b(step, far)
-        arrived(g_b.at[step], b_recv.at[step], 0)
-        prep_b(step, near)
-        particles_part(step, far)
-        send_rs(step, range(15, 7, -1))
-        particles_part(step, near)
-        send_rs(step, range(7, 0, -1))
+        wait_b(step, 0)
+        prep_b(step, 0)
+        forward(0)
+        reverse(step, 0)
+        send_back(step, 0)
+
+        @pl.when(far_group)
+        def _():
+            wait_b(step, 1)
+            prep_b(step, 1)
+            forward(1)
+
+        if step == 0:
+
+            @pl.when(n_ref < 15)
+            def _():
+                pl.semaphore_wait(ready, 15 - n_ref)
+
+        send_rs(step)
+
+        @pl.when(far_group)
+        def _():
+            reverse(step, 1)
+            send_back(step, 1)
+
         arrived(rs.at[step], rs_recv.at[step], 0)
         arrived(rs.at[step], rs_recv.at[step], 1)
         total = part[step, 0]
         for slot in range(1, 16):
             total = total + rs[step, slot]
+        wait_back(step)
+        for slot in range(1, 16):
+            total = total + g_back[step, slot]
         return total * (STEP / COUNT_P)
 
     copy_own.wait()
-    pl.semaphore_wait(barrier, 30)
+
+    @pl.when(n_dom + n_ref > 0)
+    def _():
+        pl.semaphore_wait(barrier, n_dom + n_ref)
+
     send_b(0)
+    for slot in range(15, 0, -1):
+
+        @pl.when(jnp.logical_not(ref_later[slot]))
+        def _():
+            device = {"ref": ref_partner(r, slot)}
+            pl.semaphore_signal(ready, 1, device_id=device, device_id_type=MESH)
+
     start = own[0]
     g_b[0, 0] = start
+    fill()
     copy_p.wait()
     for slot in range(16):
         rows = pl.ds(pl.multiple_of(ref_partner(r, slot) * ROWS, ROWS), ROWS)
         xs[pl.ds(slot * ROWS, ROWS), :] = p_v[rows, :]
     for rows in (near, far):
         aop[rows, :] = target_operand(xs[rows, :])
+        asop[rows, :] = source_operand(xs[rows, :])
     copy_r.wait()
     for i in range(4):
         rows = pl.ds(i * 256, 256)
@@ -209,15 +328,26 @@
         arrived(g_a, a_recv, half)
         xs[rows, :] = g_a[pl.ds(half * 8, 8)].reshape(256, WIDTH)
         aop[rows, :] = target_operand(xs[rows, :])
+        asop[rows, :] = source_operand(xs[rows, :])
         refs_part(rows)
     delta = finish(1)
     out_ref[0] = start
     out_ref[1] = now
     out_ref[2] = delta
+    for i in range(8):
+        first, size = pairs[i]
+
+        @pl.when(dom_later[i])
+        def _():
+            wait_bytes(back.at[:, pl.ds(first, size)], back_send.at[first // 2])
+
+        @pl.when(jnp.logical_not(dom_later[i]))
+        def _():
+            wait_bytes(g_b.at[:, pl.ds(first, size)], b_send.at[first // 2])
+
+    wait_bytes(g_a.at[pl.ds(1, 15)], ref_send)
     for step in range(2):
-        sent(g_b.at[step], b_send.at[step])
-        sent(rs.at[step], rs_send.at[step])
-    sent(g_a, a_send)
+        wait_bytes(rs.at[step, pl.ds(1, 15)], ref_send)
 
 
 def on_device(particles, references):
@@ -234,6 +364,8 @@
             pltpu.VMEM((BLOCK, 512), BF16),
             pltpu.VMEM((REFS, 512), BF16),
             pltpu.VMEM((NDOM * ROWS, 512), BF16),
+            pltpu.VMEM((NDOM * ROWS, 512), BF16),
+            pltpu.VMEM((BLOCK, 512), BF16),
             pltpu.VMEM((BLOCK, WIDTH), F32),
             pltpu.VMEM((BLOCK, WIDTH), F32),
             pltpu.VMEM((2, NREFD, ROWS, WIDTH), F32),
@@ -241,13 +373,17 @@
             pltpu.VMEM((2, NDOM, ROWS, WIDTH), F32),
             pltpu.VMEM((NREFD, ROWS, WIDTH), F32),
             pltpu.VMEM((2, NREFD, ROWS, WIDTH), F32),
+            pltpu.VMEM((2, NDOM, ROWS, WIDTH), F32),
+            pltpu.VMEM((2, NDOM, ROWS, WIDTH), F32),
             pltpu.SemaphoreType.DMA((3,)),
+            pltpu.SemaphoreType.DMA((8,)),
+            pltpu.SemaphoreType.DMA((2, 8)),
+            pltpu.SemaphoreType.DMA((8,)),
+            pltpu.SemaphoreType.DMA((2, 8)),
             pltpu.SemaphoreType.DMA((2,)),
+            pltpu.SemaphoreType.DMA(()),
             pltpu.SemaphoreType.DMA((2, 2)),
-            pltpu.SemaphoreType.DMA(()),
-            pltpu.SemaphoreType.DMA((2,)),
-            pltpu.SemaphoreType.DMA((2,)),
-            pltpu.SemaphoreType.DMA((2, 2)),
+            pltpu.SemaphoreType.REGULAR,
         ],
         compiler_params=pltpu.CompilerParams(
             collective_id=0, has_side_effects=True, vmem_limit_bytes=24 << 20

time: 41.7 us -> 43.8 us (1.050)
  Pallas kernels: 40.2 us -> 42.4 us
    pallas_call x1, Pallas kernels: 40.2 us -> 42.4 us  [on_device(): pl.pallas_call(kernel, out_shape=jax.ShapeDtypeStruct((3, ROWS, WIDTH), F...]
where the time goes in v4:
time: 43.8 us; the launch traced here: 43.7 us
  Pallas kernels  42.4 us (97%)
  between operations  0.64 us (1%)
  other arithmetic  0.62 us (1%)
    pallas_call x1, Pallas kernels, on_device(): pl.pallas_call(kernel, out_shape=jax.ShapeDtypeStruct((3, ROWS, WIDTH), F...  42.4 us

profile of v4, /device:TPU:1, one launch (start us, length us, event | category | flops | bytes accessed | tf_op | source)
XLA Modules:
  0.0 43.7 jit_solution(6270145435428360709)
XLA Ops:
  0.6 42.4 %flow.1 = f32[3,32,128]{2,1,0:T(8,128)S(1)} custom-call(f32[512,128]{1,0:T(8,128)} %p_hbm.1, f32[1024,128]{1,0:T(8,128)} %r_hbm.1), custom_call_target="tpu_custom_call" | custom-call | tf_op jit(solution)/shard_map/flow/pallas_call | solution.py:355
  43.0 0.6 %fusion = (f32[32,128]{1,0:T(8,128)}, f32[32,128]{1,0:T(8,128)}) fusion(f32[3,32,128]{2,1,0:T(8,128)S(1)} %flow.1), kind=kLoop, calls=%fused_computation.1 | loop fusion | flops 12288 | bytes 81920 | tf_op jit(solution)/shard_map/mul | solution.py:394

commit v5 on v3

--- a/solution.py
+++ b/solution.py
@@ -125,7 +125,8 @@
         )
 
     def send_b(step):
-        for slot in range(15, 0, -1):
+        first = [s for x in (1, 0) for s in range(15, 0, -1) if DOM_SLOTS[s][1] == x]
+        for slot in range(15, 0, -1) if step else first:
             dom_copy(own.at[step], g_b.at[step], b_send.at[step], b_recv.at[step], slot).start()
 
     def send_a():

time: 41.7 us -> 41.1 us (0.986)
  Pallas kernels: 40.2 us -> 39.7 us
    pallas_call x1, Pallas kernels: 40.2 us -> 39.7 us  [on_device(): pl.pallas_call(kernel, out_shape=jax.ShapeDtypeStruct((3, ROWS, WIDTH), F...]
where the time goes in v5:
time: 41.1 us; the launch traced here: 40.9 us
  Pallas kernels  39.7 us (97%)
  between operations  0.64 us (2%)
  other arithmetic  0.62 us (2%)
    pallas_call x1, Pallas kernels, on_device(): pl.pallas_call(kernel, out_shape=jax.ShapeDtypeStruct((3, ROWS, WIDTH), F...  39.7 us

profile of v5, /device:TPU:1, one launch (start us, length us, event | category | flops | bytes accessed | tf_op | source)
XLA Modules:
  0.0 40.9 jit_solution(12378410166998700796)
XLA Ops:
  0.6 39.7 %flow.1 = f32[3,32,128]{2,1,0:T(8,128)S(1)} custom-call(f32[512,128]{1,0:T(8,128)} %p_hbm.1, f32[1024,128]{1,0:T(8,128)} %r_hbm.1), custom_call_target="tpu_custom_call" | custom-call | tf_op jit(solution)/shard_map/flow/pallas_call | solution.py:226
  40.3 0.6 %fusion = (f32[32,128]{1,0:T(8,128)}, f32[32,128]{1,0:T(8,128)}) fusion(f32[3,32,128]{2,1,0:T(8,128)S(1)} %flow.1), kind=kLoop, calls=%fused_computation.1 | loop fusion | flops 12288 | bytes 81920 | tf_op jit(solution)/shard_map/mul | solution.py:259

commit v6 on v5

--- a/solution.py
+++ b/solution.py
@@ -98,14 +98,13 @@
     copy_own = pltpu.make_async_copy(p_hbm.at[mine], own.at[0], in_sem.at[0])
     copy_p = pltpu.make_async_copy(p_hbm, p_v, in_sem.at[1])
     copy_r = pltpu.make_async_copy(r_hbm, r_v, in_sem.at[2])
-    copy_own.start()
-    copy_p.start()
-    copy_r.start()
-
     barrier = pltpu.get_barrier_semaphore()
     for slot in range(15, 0, -1):
         device = {"dom": dom_partner(d, slot)}
         pl.semaphore_signal(barrier, 1, device_id=device, device_id_type=MESH)
+    copy_own.start()
+    copy_p.start()
+    copy_r.start()
     for slot in range(15, 0, -1):
         device = {"ref": ref_partner(r, slot)}
         pl.semaphore_signal(barrier, 1, device_id=device, device_id_type=MESH)
@@ -150,10 +149,9 @@
 
     def refs_part(rows):
         a = aop[rows, :]
-        acc, sums = pair_terms(a, rop, 0, 512)
-        acc2, sums2 = pair_terms(a, rop, 512, 512)
-        grad[rows, :] = -0.5 * (acc + acc2)
-        lanes[rows, :] = -0.5 * (sums + sums2)
+        acc, sums = pair_terms(a, rop, 0, 1024)
+        grad[rows, :] = -0.5 * acc
+        lanes[rows, :] = -0.5 * sums
 
     def particles_part(step, rows):
         acc, sums = pair_terms(aop[rows, :], sop, 0, 512)
@@ -168,9 +166,9 @@
 
     def finish(step):
         arrived(g_b.at[step], b_recv.at[step], 1)
-        prep_b(step, far)
         arrived(g_b.at[step], b_recv.at[step], 0)
-        prep_b(step, near)
+        for rows in (far, near):
+            prep_b(step, rows)
         particles_part(step, far)
         send_rs(step, range(15, 7, -1))
         particles_part(step, near)

time: 41.1 us -> 40.8 us (level)
  no operation moved by 1% of the time
where the time goes in v6:
time: 40.8 us; the launch traced here: 40.7 us
  Pallas kernels  39.4 us (97%)
  between operations  0.64 us (2%)
  other arithmetic  0.62 us (2%)
    pallas_call x1, Pallas kernels, on_device(): pl.pallas_call(kernel, out_shape=jax.ShapeDtypeStruct((3, ROWS, WIDTH), F...  39.4 us

profile of v6, /device:TPU:1, one launch (start us, length us, event | category | flops | bytes accessed | tf_op | source)
XLA Modules:
  0.0 40.7 jit_solution(16764894177621247267)
XLA Ops:
  0.6 39.4 %flow.1 = f32[3,32,128]{2,1,0:T(8,128)S(1)} custom-call(f32[512,128]{1,0:T(8,128)} %p_hbm.1, f32[1024,128]{1,0:T(8,128)} %r_hbm.1), custom_call_target="tpu_custom_call" | custom-call | tf_op jit(solution)/shard_map/flow/pallas_call | solution.py:224
  40.0 0.6 %fusion = (f32[32,128]{1,0:T(8,128)}, f32[32,128]{1,0:T(8,128)}) fusion(f32[3,32,128]{2,1,0:T(8,128)S(1)} %flow.1), kind=kLoop, calls=%fused_computation.1 | loop fusion | flops 12288 | bytes 81920 | tf_op jit(solution)/shard_map/mul | solution.py:257

commit v7 on v5

--- a/solution.py
+++ b/solution.py
@@ -129,14 +129,25 @@
         for slot in range(15, 0, -1) if step else first:
             dom_copy(own.at[step], g_b.at[step], b_send.at[step], b_recv.at[step], slot).start()
 
+    flip = {10: 12, 11: 13, 12: 10, 13: 11, 2: 4, 3: 5, 4: 2, 5: 3}
+
+    def by_core(slots, send):
+        @pl.when(r % 2 == 0)
+        def _():
+            for slot in slots:
+                send(slot)
+
+        @pl.when(r % 2 == 1)
+        def _():
+            for slot in slots:
+                send(flip.get(slot, slot))
+
     def send_a():
-        for slot in range(15, 0, -1):
-            ref_copy(own.at[1], g_a, a_send, a_recv, slot).start()
+        by_core(range(15, 0, -1), lambda slot: ref_copy(own.at[1], g_a, a_send, a_recv, slot).start())
 
     def send_rs(step, slots):
-        for slot in slots:
-            src = part.at[step, slot]
-            ref_copy(src, rs.at[step], rs_send.at[step], rs_recv.at[step], slot).start()
+        sems = rs_send.at[step], rs_recv.at[step]
+        by_core(slots, lambda slot: ref_copy(part.at[step, slot], rs.at[step], *sems, slot).start())
 
     def arrived(dst, recv, half):
         pieces = dst.at[pl.ds(1, 7)] if half == 0 else dst.at[pl.ds(8, 8)]

time: 41.1 us -> 40.8 us (level)
  no operation moved by 1% of the time
where the time goes in v7:
time: 40.8 us; the launch traced here: 40.6 us
  Pallas kernels  39.3 us (96%)
  between operations  0.64 us (2%)
  other arithmetic  0.62 us (2%)
    pallas_call x1, Pallas kernels, on_device(): pl.pallas_call(kernel, out_shape=jax.ShapeDtypeStruct((3, ROWS, WIDTH), F...  39.3 us

profile of v7, /device:TPU:1, one launch (start us, length us, event | category | flops | bytes accessed | tf_op | source)
XLA Modules:
  0.0 40.6 jit_solution(17680379714035592817)
XLA Ops:
  0.6 39.3 %flow.1 = f32[3,32,128]{2,1,0:T(8,128)S(1)} custom-call(f32[512,128]{1,0:T(8,128)} %p_hbm.1, f32[1024,128]{1,0:T(8,128)} %r_hbm.1), custom_call_target="tpu_custom_call" | custom-call | tf_op jit(solution)/shard_map/flow/pallas_call | solution.py:237
  40.0 0.6 %fusion = (f32[32,128]{1,0:T(8,128)}, f32[32,128]{1,0:T(8,128)}) fusion(f32[3,32,128]{2,1,0:T(8,128)S(1)} %flow.1), kind=kLoop, calls=%fused_computation.1 | loop fusion | flops 12288 | bytes 81920 | tf_op jit(solution)/shard_map/mul | solution.py:270

commit v8 on v7

--- a/solution.py
+++ b/solution.py
@@ -161,10 +161,9 @@
 
     def refs_part(rows):
         a = aop[rows, :]
-        acc, sums = pair_terms(a, rop, 0, 512)
-        acc2, sums2 = pair_terms(a, rop, 512, 512)
-        grad[rows, :] = -0.5 * (acc + acc2)
-        lanes[rows, :] = -0.5 * (sums + sums2)
+        acc, sums = pair_terms(a, rop, 0, 1024)
+        grad[rows, :] = -0.5 * acc
+        lanes[rows, :] = -0.5 * sums
 
     def particles_part(step, rows):
         acc, sums = pair_terms(aop[rows, :], sop, 0, 512)

time: 40.8 us -> 40.8 us (level)
  no operation moved by 1% of the time
where the time goes in v8:
time: 40.8 us; the launch traced here: 40.6 us
  Pallas kernels  39.3 us (96%)
  between operations  0.64 us (2%)
  other arithmetic  0.62 us (2%)
    pallas_call x1, Pallas kernels, on_device(): pl.pallas_call(kernel, out_shape=jax.ShapeDtypeStruct((3, ROWS, WIDTH), F...  39.3 us

profile of v8, /device:TPU:1, one launch (start us, length us, event | category | flops | bytes accessed | tf_op | source)
XLA Modules:
  0.0 40.6 jit_solution(1194641044971809035)
XLA Ops:
  0.6 39.3 %flow.1 = f32[3,32,128]{2,1,0:T(8,128)S(1)} custom-call(f32[512,128]{1,0:T(8,128)} %p_hbm.1, f32[1024,128]{1,0:T(8,128)} %r_hbm.1), custom_call_target="tpu_custom_call" | custom-call | tf_op jit(solution)/shard_map/flow/pallas_call | solution.py:236
  40.0 0.6 %fusion = (f32[32,128]{1,0:T(8,128)}, f32[32,128]{1,0:T(8,128)}) fusion(f32[3,32,128]{2,1,0:T(8,128)S(1)} %flow.1), kind=kLoop, calls=%fused_computation.1 | loop fusion | flops 12288 | bytes 81920 | tf_op jit(solution)/shard_map/mul | solution.py:269
